TPU v7x, 512 devices: a whole 4x8x8 slice. The times are simulated.
512 devices in a mesh: tile: 32 (over y, x), tm: 16 (over z, core).
Axes of the slice: x: 4, y: 8, z: 8, core: 2. Of those that a mesh axis runs over, the one named last changes fastest.
Arguments:
- movie: bfloat16 [256, 256, 4096], P('tm', None, 'tile'), may hold values from -6 to 6
- omega: bfloat16 [2, 32, 32, 256], P(None, 'tile', None, 'tm'), may hold values from -0.375 to 0.375
- time_taps: bfloat16 [17], replicated, may hold values from 0.019897461 to 0.099609375
- space_taps: bfloat16 [17], replicated, may hold values from 0.099609375 to 0.29882812
Outputs:
- basis: float32 [32, 256, 4096], P(None, 'tm', 'tile')
- coefficients: float32 [2, 32, 32, 256], P(None, 'tile', None, 'tm')
All inputs are finite; a program needn't handle non-finite values.
Results may differ from a plain program's by a relative error of at most 0.024.
Values may be sent and summed in bfloat16 or wider, within the bound.
A program may use at most 64 MiB of HBM per device.

v0:
```python
import math
import jax
import jax.numpy as jnp
from jax import lax
from jax.sharding import PartitionSpec as P

H = 128
TY = 2


def with_halo(block, sides, width):
    for axis, dim in sides:
        count = lax.axis_size(axis)
        forward = [(i, i + 1) for i in range(count - 1)]
        backward = [(target, source) for source, target in forward]
        low = lax.ppermute(
            lax.slice_in_dim(block, block.shape[dim] - width, None, axis=dim), axis, forward
        )
        high = lax.ppermute(lax.slice_in_dim(block, 0, width, axis=dim), axis, backward)
        block = jnp.concatenate([low, block, high], axis=dim)
    return block


def band(tap_row, out_count, in_count, offset_by):
    row_ids = lax.broadcasted_iota(jnp.int32, (out_count, in_count), 0)
    col_ids = lax.broadcasted_iota(jnp.int32, (out_count, in_count), 1)
    offsets = col_ids - row_ids + offset_by
    picks = jnp.arange(tap_row.shape[0], dtype=jnp.int32)
    hits = (offsets[:, :, None] == picks).astype(jnp.float32)
    return jnp.sum(hits * tap_row.astype(jnp.float32), axis=2).astype(jnp.bfloat16)


def orthonormal(matrix):
    gram_block = jnp.dot(matrix, matrix.T, precision=lax.Precision.HIGHEST)
    factor_low = jnp.linalg.cholesky(gram_block)
    return jax.scipy.linalg.solve_triangular(factor_low, matrix, lower=True)


def local(movie, omega, time_taps, space_taps):
    frames, image_rows, tile_cols = movie.shape
    radius = (time_taps.shape[0] - 1) // 2
    tile_rows = H
    stack = TY
    pixels = tile_rows * tile_cols
    rank_count = omega.shape[2]
    row_share = image_rows // lax.axis_size("tm")
    time_band = band(time_taps, frames, frames + 2 * radius, 0)
    padded = with_halo(movie, (("tm", 0),), radius)
    flat_rows = padded.reshape(frames + 2 * radius, image_rows * tile_cols)
    low_time = jnp.dot(time_band, flat_rows, preferred_element_type=jnp.float32)
    centre = flat_rows[radius : radius + frames].astype(jnp.float32)
    temporal = (centre - low_time).astype(jnp.bfloat16).reshape(frames, image_rows, tile_cols)
    temporal = with_halo(temporal, (("tile", 2),), radius)
    across = band(space_taps, tile_cols, tile_cols + 2 * radius, 0).T
    smooth_x = jnp.dot(temporal, across, preferred_element_type=jnp.float32).astype(jnp.bfloat16)
    down_band = band(space_taps, image_rows, image_rows, radius)
    lowpass = jnp.einsum("ab,fbw->faw", down_band, smooth_x, preferred_element_type=jnp.float32)
    centre_z = temporal[:, :, radius : radius + tile_cols].astype(jnp.float32)
    filtered = (centre_z - lowpass).astype(jnp.bfloat16).reshape(frames, stack, pixels)
    row_start = lax.axis_index("tm") * row_share

    def to_image(tiled):
        shaped = tiled.reshape(stack, rank_count, tile_rows, tile_cols)
        return jnp.transpose(shaped, (1, 0, 2, 3)).reshape(rank_count, image_rows, tile_cols)

    def subspace(partial_value):
        summed = lax.psum(partial_value.astype(jnp.bfloat16), "tm").astype(jnp.float32)
        basis_all = jax.vmap(orthonormal)(summed)
        own_rows = lax.dynamic_slice_in_dim(to_image(basis_all), row_start, row_share, 1)
        return (basis_all.astype(jnp.bfloat16), own_rows)

    omega_local = omega[:, 0]
    sketch = jnp.einsum("tkf,ftp->tkp", omega_local, filtered, preferred_element_type=jnp.float32)
    first_basis, unused_rows = subspace(sketch)
    loadings = jnp.einsum(
        "ftp,tkp->ftk", filtered, first_basis, preferred_element_type=jnp.float32
    ).astype(jnp.bfloat16)
    refined = jnp.einsum("ftk,ftp->tkp", loadings, filtered, preferred_element_type=jnp.float32)
    final_basis, final_rows = subspace(refined)
    coefficients = jnp.einsum(
        "tkp,ftp->tkf", final_basis, filtered, preferred_element_type=jnp.float32
    )
    return (final_rows * math.sqrt(pixels), coefficients[:, None])


def solution(mesh):
    in_specs = (P("tm", None, "tile"), P(None, "tile", None, "tm"), P(), P())
    out_specs = (P(None, "tm", "tile"), P(None, "tile", None, "tm"))
    return jax.shard_map(local, mesh=mesh, in_specs=in_specs, out_specs=out_specs, check_vma=False)
```

profile of v0, /device:TPU:1, one launch (start us, length us, event | category | flops | bytes accessed | tf_op | source)
XLA Modules:
  0.0 342.5 jit_solution(9455576074152000294)
XLA Ops:
  7.2 1.4 fusion.46
  8.6 5.4 %collective-permute-start = (bf16[8,256,128]{2,1,0:T(8,128)(2,1)S(1)}, bf16[8,256,128]{2,1,0:T(8,128)(2,1)S(1)}, u32[]{:S(2)}, u32[]{:S(2)}) collective-permute-start(bf16[8,256,128]{2,1,0:T(8,128)(2,1)S(1)} %get-tuple-element.14), channel_id=1, source_target_pairs={{0,1},{1,2},{2,3},{3,4},{4,5},{5,6},{6,7},{7,8},{8,9},{9,10},{10,1... | collective-permute-start | bytes 1572872 | tf_op jit(solution)/shard_map/ppermute | solution.py:16
  14.0 4.7 %collective-permute-start.1 = (bf16[8,256,128]{2,1,0:T(8,128)(2,1)S(1)}, bf16[8,256,128]{2,1,0:T(8,128)(2,1)S(1)}, u32[]{:S(2)}, u32[]{:S(2)}) collective-permute-start(bf16[8,256,128]{2,1,0:T(8,128)(2,1)S(1)} %get-tuple-element.15), channel_id=1, source_target_pairs={{1,0},{2,1},{3,2},{4,3},{5,4},{6,5},{7,6},{8,7},{9,8},{10,9},{11,1... | collective-permute-start | bytes 1572872 | tf_op jit(solution)/shard_map/ppermute | solution.py:19
  19.2 0.5 select_reduce_fusion
  19.7 0.5 collective-permute-done
  20.1 4.4 %collective-permute-done.1 = bf16[8,256,128]{2,1,0:T(8,128)(2,1)S(1)} collective-permute-done((bf16[8,256,128]{2,1,0:T(8,128)(2,1)S(1)}, bf16[8,256,128]{2,1,0:T(8,128)(2,1)S(1)}, u32[]{:S(2)}, u32[]{:S(2)}) %collective-permute-start.1) | collective-permute-done | bytes 524320 | tf_op jit(solution)/shard_map/ppermute | solution.py:19
  24.5 0.2 pad_maximum_fusion
  24.8 2.3 fusion.10
  27.3 0.5 copy.38
  27.8 3.1 collective-permute-start.2
  31.0 1.3 collective-permute-start.3
  32.5 3.5 %collective-permute-done.3 = bf16[16,256,8]{1,2,0:T(8,128)(2,1)S(1)} collective-permute-done((bf16[16,256,8]{1,2,0:T(8,128)(2,1)S(1)}, bf16[16,256,8]{1,2,0:T(8,128)(2,1)S(1)}, u32[]{:S(2)}, u32[]{:S(2)}) %collective-permute-start.3) | collective-permute-done | bytes 65568 | tf_op jit(solution)/shard_map/ppermute | solution.py:19
  36.0 1.5 fusion.7
  37.5 0.7 copy.43
  38.2 0.3 reshape.57
  38.5 2.6 fusion.1
  41.2 127.3 %all-reduce.3.cloned.1.call-done = bf16[2,32,16384]{2,1,0:T(8,128)(2,1)} async-done(((bf16[2,32,16384]{2,1,0:T(8,128)(2,1)}), bf16[2,32,16384]{2,1,0:T(8,128)(2,1)}) %all-reduce.3.cloned.1.call-update) | async-done | bytes 2097168 | tf_op jit(solution)/shard_map/psum | solution.py:67
  168.6 3.0 fusion.47
  171.7 6.0 %custom-call.8 = f32[2,32,32]{2,1,0:T(8,128)S(1)} custom-call(f32[2,32,32]{2,1,0:T(8,128)S(1)} %fusion.40), custom_call_target="Cholesky" | custom-call | tf_op jit(solution)/shard_map/vmap(jit(cholesky))/cholesky | solution.py:35
  178.0 4.9 %custom-call.9 = f32[2,1,32,32]{2,3,1,0:T(8,128)S(1)} custom-call(f32[2,1,32,32]{3,2,1,0:T(8,128)S(1)} %select_bitcast_fusion.1), custom_call_target="InvertDiagBlocksLowerTriangular" | custom-call | tf_op jit(solution)/shard_map/vmap(jit(_solve_triangular))/triangular_solve | solution.py:36
  182.9 4.8 %convolution_convert_fusion.1 = bf16[2,32,16384]{2,1,0:T(8,128)(2,1)} fusion(bf16[2,32,16384]{2,1,0:T(8,128)(2,1)S(1)} %copy-done.2, f32[2,1,32,32]{2,3,1,0:T(8,128)S(1)} %custom-call.9), kind=kOutput, calls=%fused_computation.3 | convolution fusion | flops 404750336 | bytes 4202496 | tf_op jit(solution)/shard_map/vmap(jit(_solve_triangular))/triangular_solve | solution.py:36
  187.7 5.3 %convolution_convert_fusion = bf16[2,32,16384]{2,1,0:T(8,128)(2,1)} fusion(bf16[2,32,16384]{2,1,0:T(8,128)(2,1)} %convolution_convert_fusion.1, bf16[16,2,16384]{2,1,0:T(2,128)(2,1)S(1)} %reshape.57), kind=kOutput, calls=%fused_computation.2 | convolution fusion | flops 68158464 | bytes 5242880 | tf_op jit(solution)/shard_map/ftk,ftp->tkp/dot_general | solution.py:78
  193.0 120.7 %all-reduce.5.cloned.1.call-done = bf16[2,32,16384]{2,1,0:T(8,128)(2,1)} async-done(((bf16[2,32,16384]{2,1,0:T(8,128)(2,1)}), bf16[2,32,16384]{2,1,0:T(8,128)(2,1)}) %all-reduce.5.cloned.1.call-update) | async-done | bytes 2097168 | tf_op jit(solution)/shard_map/psum | solution.py:67
  313.7 3.0 fusion.48
  316.8 5.9 %custom-call.10 = f32[2,32,32]{2,1,0:T(8,128)S(1)} custom-call(f32[2,32,32]{2,1,0:T(8,128)S(1)} %fusion.38), custom_call_target="Cholesky" | custom-call | tf_op jit(solution)/shard_map/vmap(jit(cholesky))/cholesky | solution.py:35
  322.9 4.9 %custom-call.11 = f32[2,1,32,32]{2,3,1,0:T(8,128)S(1)} custom-call(f32[2,1,32,32]{3,2,1,0:T(8,128)S(1)} %select_bitcast_fusion), custom_call_target="InvertDiagBlocksLowerTriangular" | custom-call | tf_op jit(solution)/shard_map/vmap(jit(_solve_triangular))/triangular_solve | solution.py:36
  327.9 3.9 %fusion.2 = f32[2,32,16384]{2,1,0:T(8,128)S(1)} fusion(bf16[2,32,16384]{2,1,0:T(8,128)(2,1)S(1)} %copy-done.1, f32[2,1,32,32]{2,3,1,0:T(8,128)S(1)} %custom-call.11), kind=kOutput, calls=%fused_computation.9 | convolution fusion | flops 403701760 | bytes 6299648 | tf_op jit(solution)/shard_map/vmap(jit(_solve_triangular))/triangular_solve | solution.py:36
  331.7 1.5 fusion.23
  333.2 0.7 copy.60
  333.9 0.5 bitcast_bitcast_fusion
  334.4 0.5 copy.51
  334.9 0.7 dynamic-slice_multiply_fusion
  (39 shorter events, 1.5 us)
Async XLA Ops:
  7.2 31.3 %copy-start = (bf16[2,1,32,16]{2,3,1,0:T(8,128)(2,1)S(1)}, bf16[2,1,32,16]{2,3,1,0:T(8,128)(2,1)}, u32[]{:S(2)}) copy-start(bf16[2,1,32,16]{2,3,1,0:T(8,128)(2,1)} %param.8) | copy-start | bytes 6148
  7.2 11.6 %copy-start.3 = (bf16[16,256,128]{2,1,0:T(8,128)(2,1)S(1)}, bf16[16,256,128]{2,1,0:T(8,128)(2,1)}, u32[]{:S(2)}) copy-start(bf16[16,256,128]{2,1,0:T(8,128)(2,1)} %param.7) | copy-start | bytes 3145732
  7.2 161.4 %all-reduce.3.cloned.1.call-start = ((), (), s32[]{:S(2)}) async-start(), calls=%async_computation | async-start | bytes 4194304 | tf_op jit(solution)/shard_map/psum | solution.py:67
  8.6 10.4 %copy-start.4 = (bf16[17]{0:T(256)(128)(2,1)S(1)}, bf16[17]{0:T(256)(128)(2,1)}, u32[]{:S(2)}) copy-start(bf16[17]{0:T(256)(128)(2,1)} %param.9) | copy-start | bytes 106
  8.6 10.4 %copy-start.5 = (bf16[17]{0:T(256)(128)(2,1)S(1)}, bf16[17]{0:T(256)(128)(2,1)}, u32[]{:S(2)}) copy-start(bf16[17]{0:T(256)(128)(2,1)} %param.10) | copy-start | bytes 106
  8.6 11.5 %collective-permute-start = (bf16[8,256,128]{2,1,0:T(8,128)(2,1)S(1)}, bf16[8,256,128]{2,1,0:T(8,128)(2,1)S(1)}, u32[]{:S(2)}, u32[]{:S(2)}) collective-permute-start(bf16[8,256,128]{2,1,0:T(8,128)(2,1)S(1)} %get-tuple-element.14), channel_id=1, source_target_pairs={{0,1},{1,2},{2,3},{3,4},{4,5},{5,6},{6,7},{7,8},{8,9},{9,10},{10,1... | collective-permute-start | bytes 1572872 | tf_op jit(solution)/shard_map/ppermute | solution.py:16
  14.0 10.5 %collective-permute-start.1 = (bf16[8,256,128]{2,1,0:T(8,128)(2,1)S(1)}, bf16[8,256,128]{2,1,0:T(8,128)(2,1)S(1)}, u32[]{:S(2)}, u32[]{:S(2)}) collective-permute-start(bf16[8,256,128]{2,1,0:T(8,128)(2,1)S(1)} %get-tuple-element.15), channel_id=1, source_target_pairs={{1,0},{2,1},{3,2},{4,3},{5,4},{6,5},{7,6},{8,7},{9,8},{10,9},{11,1... | collective-permute-start | bytes 1572872 | tf_op jit(solution)/shard_map/ppermute | solution.py:19
  27.8 4.6 %collective-permute-start.2 = (bf16[16,256,8]{1,2,0:T(8,128)(2,1)S(1)}, bf16[16,256,8]{1,2,0:T(8,128)(2,1)S(1)}, u32[]{:S(2)}, u32[]{:S(2)}) collective-permute-start(bf16[16,256,8]{1,2,0:T(8,128)(2,1)S(1)} %get-tuple-element.12), channel_id=1, source_target_pairs={{0,16},{16,32},{32,48},{48,64},{64,80},{80,96},{96,112},{112,128},... | collective-permute-start | bytes 196616 | tf_op jit(solution)/shard_map/ppermute | solution.py:16
  31.0 5.0 %collective-permute-start.3 = (bf16[16,256,8]{1,2,0:T(8,128)(2,1)S(1)}, bf16[16,256,8]{1,2,0:T(8,128)(2,1)S(1)}, u32[]{:S(2)}, u32[]{:S(2)}) collective-permute-start(bf16[16,256,8]{1,2,0:T(8,128)(2,1)S(1)} %get-tuple-element.13), channel_id=1, source_target_pairs={{16,0},{32,16},{48,32},{64,48},{80,64},{96,80},{112,96},{128,112},... | collective-permute-start | bytes 196616 | tf_op jit(solution)/shard_map/ppermute | solution.py:19
  41.2 272.5 %all-reduce.5.cloned.1.call-start = ((), (), s32[]{:S(2)}) async-start(), calls=%async_computation.1 | async-start | bytes 4194304 | tf_op jit(solution)/shard_map/psum | solution.py:67
  168.6 14.3 %copy-start.2 = (bf16[2,32,16384]{2,1,0:T(8,128)(2,1)S(1)}, bf16[2,32,16384]{2,1,0:T(8,128)(2,1)}, u32[]{:S(2)}) copy-start(bf16[2,32,16384]{2,1,0:T(8,128)(2,1)} %all-reduce.3.cloned.1.call-done) | copy-start | bytes 6291460
  313.7 14.2 %copy-start.1 = (bf16[2,32,16384]{2,1,0:T(8,128)(2,1)S(1)}, bf16[2,32,16384]{2,1,0:T(8,128)(2,1)}, u32[]{:S(2)}) copy-start(bf16[2,32,16384]{2,1,0:T(8,128)(2,1)} %all-reduce.5.cloned.1.call-done) | copy-start | bytes 6291460
Sparse Core Ops, SparseCore 0:
  41.3 127.2 all-reduce.2
  193.1 120.5 all-reduce.4
where the time goes:
time: 343 us; the launch traced here: 342 us
  waiting for transfers between devices  256 us (75%)
  matrix products  27.9 us (8%)
  other arithmetic  24.2 us (7%)
  starting transfers between devices  14.6 us (4%)
  between operations  14.3 us (4%)
  local copies, waits for them, and re-layouts  4.95 us (1%)
    psum x2, waiting for transfers between devices, subspace(): lax.psum(partial_value.astype(jnp.bfloat16), 'tm').astype(jnp.float32)  248 us
    another operation x7, other arithmetic, orthonormal(): factor_low = jnp.linalg.cholesky(gram_block)  12.2 us
    another operation x5, other arithmetic, orthonormal(): return jax.scipy.linalg.solve_triangular(factor_low, matrix, lower=True)  9.99 us
    another operation x2, matrix products, orthonormal(): return jax.scipy.linalg.solve_triangular(factor_low, matrix, lower=True)  8.65 us
    ppermute x2, starting transfers between devices, with_halo(): lax.ppermute(lax.slice_in_dim(block, block.shape[dim] - width, None, axis...  8.51 us
    ppermute x2, waiting for transfers between devices, with_halo(): lax.ppermute(lax.slice_in_dim(block, 0, width, axis=dim), axis, backward)  7.9 us
  transfers between devices with their start and end apart: 6, of which 5 were waited for; matrix products, arithmetic and copies ran while one was open for 0% of the time, Pallas kernels for 0%

commit v1 on v0

--- a/solution.py
+++ b/solution.py
@@ -64,7 +64,9 @@
         return jnp.transpose(shaped, (1, 0, 2, 3)).reshape(rank_count, image_rows, tile_cols)
 
     def subspace(partial_value):
-        summed = lax.psum(partial_value.astype(jnp.bfloat16), "tm").astype(jnp.float32)
+        summed = jnp.sum(
+            lax.all_gather(partial_value.astype(jnp.bfloat16), axis_name="tm"), axis=0
+        ).astype(jnp.float32)
         basis_all = jax.vmap(orthonormal)(summed)
         own_rows = lax.dynamic_slice_in_dim(to_image(basis_all), row_start, row_share, 1)
         return (basis_all.astype(jnp.bfloat16), own_rows)

time: 343 us -> 474 us (1.38)
  waiting for transfers between devices: 256 us -> 369 us
  other arithmetic: 24.2 us -> 47.5 us
    all_gather x0 -> x2, waiting for transfers between devices: none -> 361 us  [subspace(): lax.all_gather(partial_value.astype(jnp.bfloat16), axis_name='tm')]
    psum x2 -> x0, waiting for transfers between devices: 248 us -> none  [subspace(): lax.psum(partial_value.astype(jnp.bfloat16), 'tm').astype(jnp.float32)]
    reduce_sum x0 -> x2, other arithmetic: none -> 23.3 us  [subspace(): jnp.sum(lax.all_gather(partial_value.astype(jnp.bfloat16), axis_name='tm'...]
    dot_general x2, matrix products: 6.08 us -> 1.34 us  [orthonormal(): gram_block = jnp.dot(matrix, matrix.T, precision=lax.Precision.HIGHEST)]
where the time goes in v1:
time: 474 us
  waiting for transfers between devices  369 us (78%)
  other arithmetic  47.5 us (10%)
  matrix products  23.2 us (5%)
  starting transfers between devices  14.8 us (3%)
  between operations  14.4 us (3%)
  local copies, waits for them, and re-layouts  4.94 us (1%)
    all_gather x2, waiting for transfers between devices, subspace(): lax.all_gather(partial_value.astype(jnp.bfloat16), axis_name='tm')  361 us
    reduce_sum x2, other arithmetic, subspace(): jnp.sum(lax.all_gather(partial_value.astype(jnp.bfloat16), axis_name='tm'...  23.3 us
    another operation x7, other arithmetic, orthonormal(): factor_low = jnp.linalg.cholesky(gram_block)  12 us
    another operation x5, other arithmetic, orthonormal(): return jax.scipy.linalg.solve_triangular(factor_low, matrix, lower=True)  10.2 us
  transfers between devices with their start and end apart: 6, of which 5 were waited for; matrix products, arithmetic and copies ran while one was open for 0% of the time, Pallas kernels for 0%

profile of v1, /device:TPU:1, one launch (start us, length us, event | category | flops | bytes accessed | tf_op | source)
XLA Modules:
  0.0 473.8 jit_solution(10413780454010770378)
XLA Ops:
  7.2 1.4 fusion.46
  8.6 5.4 %collective-permute-start = (bf16[8,256,128]{2,1,0:T(8,128)(2,1)S(1)}, bf16[8,256,128]{2,1,0:T(8,128)(2,1)S(1)}, u32[]{:S(2)}, u32[]{:S(2)}) collective-permute-start(bf16[8,256,128]{2,1,0:T(8,128)(2,1)S(1)} %get-tuple-element.14), channel_id=1, source_target_pairs={{0,1},{1,2},{2,3},{3,4},{4,5},{5,6},{6,7},{7,8},{8,9},{9,10},{10,1... | collective-permute-start | bytes 1572872 | tf_op jit(solution)/shard_map/ppermute | solution.py:16
  14.0 4.7 collective-permute-start.1
  19.2 0.5 select_reduce_fusion
  19.7 0.5 collective-permute-done
  20.1 4.4 collective-permute-done.1
  24.8 2.3 fusion.10
  27.3 0.5 copy.38
  27.8 3.1 collective-permute-start.2
  31.0 1.3 collective-permute-start.3
  32.5 3.5 collective-permute-done.3
  36.0 1.5 fusion.7
  37.5 0.7 copy.43
  38.5 2.7 fusion.1
  41.4 184.6 %all-gather.5.cloned.1.call-done = bf16[32,32,16384]{2,1,0:T(8,128)(2,1)} async-done(((bf16[2,32,16384]{2,1,0:T(8,128)(2,1)}), bf16[32,32,16384]{2,1,0:T(8,128)(2,1)}) %all-gather.5.cloned.1.call-update) | async-done | bytes 33554448 | tf_op jit(solution)/shard_map/all_gather | solution.py:68
  226.1 11.6 %reduce_sum.54 = bf16[2,32,16384]{2,1,0:T(8,128)(2,1)S(1)} reduce(bf16[16,2,32,16384]{3,2,1,0:T(8,128)(2,1)} %bitcast.76, bf16[]{:T(256)} %constant.48.clone.1), dimensions={0}, to_apply=%region_3.0 | reduce | flops 15728640 | bytes 35651584 | tf_op jit(solution)/shard_map/reduce_sum | solution.py:67
  237.7 0.7 fusion.47
  238.5 5.9 %custom-call.8 = f32[2,32,32]{2,1,0:T(8,128)S(1)} custom-call(f32[2,32,32]{2,1,0:T(8,128)S(1)} %fusion.40), custom_call_target="Cholesky" | custom-call | tf_op jit(solution)/shard_map/vmap(jit(cholesky))/cholesky | solution.py:35
  244.6 4.9 %custom-call.9 = f32[2,1,32,32]{2,3,1,0:T(8,128)S(1)} custom-call(f32[2,1,32,32]{3,2,1,0:T(8,128)S(1)} %select_bitcast_fusion.1), custom_call_target="InvertDiagBlocksLowerTriangular" | custom-call | tf_op jit(solution)/shard_map/vmap(jit(_solve_triangular))/triangular_solve | solution.py:36
  249.5 4.8 %convolution_convert_fusion.1 = bf16[2,32,16384]{2,1,0:T(8,128)(2,1)} fusion(bf16[2,32,16384]{2,1,0:T(8,128)(2,1)S(1)} %reduce_sum.54, f32[2,1,32,32]{2,3,1,0:T(8,128)S(1)} %custom-call.9), kind=kOutput, calls=%fused_computation.3 | convolution fusion | flops 404750336 | bytes 4202496 | tf_op jit(solution)/shard_map/vmap(jit(_solve_triangular))/triangular_solve | solution.py:36
  254.3 5.2 %convolution_convert_fusion = bf16[2,32,16384]{2,1,0:T(8,128)(2,1)} fusion(bf16[2,32,16384]{2,1,0:T(8,128)(2,1)} %convolution_convert_fusion.1, bf16[16,2,16384]{2,1,0:T(2,128)(2,1)S(1)} %reshape.57), kind=kOutput, calls=%fused_computation.2 | convolution fusion | flops 68158464 | bytes 5242880 | tf_op jit(solution)/shard_map/ftk,ftp->tkp/dot_general | solution.py:80
  259.6 175.9 %all-gather.7.cloned.1.call-done = bf16[32,32,16384]{2,1,0:T(8,128)(2,1)} async-done(((bf16[2,32,16384]{2,1,0:T(8,128)(2,1)}), bf16[32,32,16384]{2,1,0:T(8,128)(2,1)}) %all-gather.7.cloned.1.call-update) | async-done | bytes 33554448 | tf_op jit(solution)/shard_map/all_gather | solution.py:68
  435.5 11.6 %reduce_sum.55 = bf16[2,32,16384]{2,1,0:T(8,128)(2,1)S(1)} reduce(bf16[16,2,32,16384]{3,2,1,0:T(8,128)(2,1)} %bitcast.75, bf16[]{:T(256)} %constant.48.clone.1), dimensions={0}, to_apply=%region_6.9 | reduce | flops 15728640 | bytes 35651584 | tf_op jit(solution)/shard_map/reduce_sum | solution.py:67
  447.2 0.7 fusion.48
  447.9 5.9 %custom-call.10 = f32[2,32,32]{2,1,0:T(8,128)S(1)} custom-call(f32[2,32,32]{2,1,0:T(8,128)S(1)} %fusion.38), custom_call_target="Cholesky" | custom-call | tf_op jit(solution)/shard_map/vmap(jit(cholesky))/cholesky | solution.py:35
  454.0 5.1 %custom-call.11 = f32[2,1,32,32]{2,3,1,0:T(8,128)S(1)} custom-call(f32[2,1,32,32]{3,2,1,0:T(8,128)S(1)} %select_bitcast_fusion), custom_call_target="InvertDiagBlocksLowerTriangular" | custom-call | tf_op jit(solution)/shard_map/vmap(jit(_solve_triangular))/triangular_solve | solution.py:36
  459.2 3.8 fusion.2
  463.0 1.5 fusion.23
  464.5 0.7 copy.60
  465.2 0.5 bitcast_bitcast_fusion
  465.7 0.5 copy.51
  466.2 0.7 dynamic-slice_multiply_fusion
  (39 shorter events, 2.2 us)
Async XLA Ops:
  7.2 31.3 %copy-start = (bf16[2,1,32,16]{2,3,1,0:T(8,128)(2,1)S(1)}, bf16[2,1,32,16]{2,3,1,0:T(8,128)(2,1)}, u32[]{:S(2)}) copy-start(bf16[2,1,32,16]{2,3,1,0:T(8,128)(2,1)} %param.8) | copy-start | bytes 6148
  7.2 11.6 %copy-start.2 = (bf16[16,256,128]{2,1,0:T(8,128)(2,1)S(1)}, bf16[16,256,128]{2,1,0:T(8,128)(2,1)}, u32[]{:S(2)}) copy-start(bf16[16,256,128]{2,1,0:T(8,128)(2,1)} %param.7) | copy-start | bytes 3145732
  7.2 218.9 %all-gather.5.cloned.1.call-start = ((), (), s32[]{:S(2)}) async-start(), calls=%async_computation | async-start | bytes 35651584 | tf_op jit(solution)/shard_map/all_gather | solution.py:68
  8.6 10.4 %copy-start.3 = (bf16[17]{0:T(256)(128)(2,1)S(1)}, bf16[17]{0:T(256)(128)(2,1)}, u32[]{:S(2)}) copy-start(bf16[17]{0:T(256)(128)(2,1)} %param.9) | copy-start | bytes 106
  8.6 10.4 %copy-start.4 = (bf16[17]{0:T(256)(128)(2,1)S(1)}, bf16[17]{0:T(256)(128)(2,1)}, u32[]{:S(2)}) copy-start(bf16[17]{0:T(256)(128)(2,1)} %param.10) | copy-start | bytes 106
  8.6 11.5 %collective-permute-start = (bf16[8,256,128]{2,1,0:T(8,128)(2,1)S(1)}, bf16[8,256,128]{2,1,0:T(8,128)(2,1)S(1)}, u32[]{:S(2)}, u32[]{:S(2)}) collective-permute-start(bf16[8,256,128]{2,1,0:T(8,128)(2,1)S(1)} %get-tuple-element.14), channel_id=1, source_target_pairs={{0,1},{1,2},{2,3},{3,4},{4,5},{5,6},{6,7},{7,8},{8,9},{9,10},{10,1... | collective-permute-start | bytes 1572872 | tf_op jit(solution)/shard_map/ppermute | solution.py:16
  14.0 10.5 %collective-permute-start.1 = (bf16[8,256,128]{2,1,0:T(8,128)(2,1)S(1)}, bf16[8,256,128]{2,1,0:T(8,128)(2,1)S(1)}, u32[]{:S(2)}, u32[]{:S(2)}) collective-permute-start(bf16[8,256,128]{2,1,0:T(8,128)(2,1)S(1)} %get-tuple-element.15), channel_id=1, source_target_pairs={{1,0},{2,1},{3,2},{4,3},{5,4},{6,5},{7,6},{8,7},{9,8},{10,9},{11,1... | collective-permute-start | bytes 1572872 | tf_op jit(solution)/shard_map/ppermute | solution.py:19
  27.8 4.6 collective-permute-start.2
  31.0 5.0 %collective-permute-start.3 = (bf16[16,256,8]{1,2,0:T(8,128)(2,1)S(1)}, bf16[16,256,8]{1,2,0:T(8,128)(2,1)S(1)}, u32[]{:S(2)}, u32[]{:S(2)}) collective-permute-start(bf16[16,256,8]{1,2,0:T(8,128)(2,1)S(1)} %get-tuple-element.13), channel_id=1, source_target_pairs={{16,0},{32,16},{48,32},{64,48},{80,64},{96,80},{112,96},{128,112},... | collective-permute-start | bytes 196616 | tf_op jit(solution)/shard_map/ppermute | solution.py:19
  41.2 394.4 %all-gather.7.cloned.1.call-start = ((), (), s32[]{:S(2)}) async-start(), calls=%async_computation.1 | async-start | bytes 35651584 | tf_op jit(solution)/shard_map/all_gather | solution.py:68
  465.7 1.2 copy-start.1
Sparse Core Ops, SparseCore 0:
  41.3 184.7 all-gather.4
  259.7 175.7 all-gather.6
